TPU v7x, 512 devices: a whole 4x8x8 slice. The times are simulated.
512 devices in a mesh: grp: 16 (over y, core), mdl: 32 (over x, z).
Axes of the slice: x: 4, y: 8, z: 8, core: 2. Of those that a mesh axis runs over, the one named last changes fastest.
Arguments:
- row_states: bfloat16 [6144, 1024], P('grp', 'mdl'), may hold values from -6 to 6
- ffn_gain: bfloat16 [1024], replicated, may hold values from 0.25 to 1.75
- ffn_in: bfloat16 [1024, 32768], P('grp', 'mdl'), may hold values from -0.1875 to 0.1875
- ffn_out: bfloat16 [32768, 1024], P('mdl', 'grp'), may hold values from -0.0625 to 0.0625
- final_gain: bfloat16 [1024], replicated, may hold values from 0.25 to 1.75
- kv_weight: bfloat16 [2, 1024, 16384], P(None, None, 'mdl'), may hold values from -0.1875 to 0.1875
- queries: bfloat16 [4096, 16384], P('grp', 'mdl'), may hold values from -36 to 36
- attn_out: bfloat16 [16384, 1024], P('mdl'), may hold values from -0.75 to 0.75
- row_question: int32 [6144], replicated, may hold values from 0 to 15, as said below
Outputs:
- cross_out: bfloat16 [4096, 1024], P(('grp', 'mdl'))
Inputs may be any that keep to these rules, and one draw needn't show every extreme that they name: `row_question`: within each block of 384 rows (one row group) the rows are sorted by question; in every block each question owns a multiple of 8 rows, at least 8 and at most 72, and one question, drawn from the seed, owns exactly 72 rows of every block.
All inputs are finite; a program needn't handle non-finite values.
Results may differ from a plain program's by a relative error of at most 0.029.
Values may be sent and summed in bfloat16 or wider, within the bound.
No kernel may reach another device: no remote copies, remote signals or barrier semaphores. Data moves between devices by JAX's collectives and lax.ppermute only.
A program may use at most 64 MiB of HBM per device.

v0:
```python
import jax
import jax.numpy as jnp
from jax import lax
from jax.sharding import PartitionSpec as P

HEAD_DIM = 128


def rms_normalize(states, gain):
    wide = states.astype(jnp.float32)
    factor = lax.rsqrt(jnp.mean(wide * wide, axis=-1, keepdims=True) + 1e-06)
    return (wide * factor * gain.astype(jnp.float32)).astype(jnp.bfloat16)


def bucket_plan(row_question, rows_local, groups, my_group):
    capacity = 3 * rows_local // groups
    owners = row_question.reshape(groups, rows_local)
    owner_table = (owners[:, :, None] == jnp.arange(groups, dtype=jnp.int32)[None, None, :]).astype(
        jnp.int32
    )
    counts = jnp.sum(owner_table, axis=1)
    starts = jnp.cumsum(counts, axis=1) - counts
    slot_index = jnp.arange(capacity, dtype=jnp.int32)
    sent_counts = lax.dynamic_index_in_dim(counts, my_group, 0, keepdims=False)
    sent_starts = lax.dynamic_index_in_dim(starts, my_group, 0, keepdims=False)
    send_valid = slot_index[None, :] < sent_counts[:, None]
    send_rows = jnp.minimum(sent_starts[:, None] + slot_index[None, :], rows_local - 1)
    got_counts = lax.dynamic_index_in_dim(counts, my_group, 1, keepdims=False)
    got_valid = (slot_index[None, :] < got_counts[:, None]).reshape(-1)
    return (capacity, send_rows, send_valid, got_valid)


def pack_slots(source, send_rows, send_valid):
    picked = jnp.take(source, send_rows.reshape(-1), axis=0)
    picked = picked.reshape(send_rows.shape[0], send_rows.shape[1], source.shape[1])
    picked = jnp.where(send_valid[:, :, None], picked, jnp.zeros((), source.dtype))
    return picked.reshape(send_rows.shape[0], -1)


def local(
    row_states, ffn_gain, ffn_in, ffn_out, final_gain, kv_weight, queries, attn_out, row_question
):
    groups = lax.axis_size("grp")
    my_group = lax.axis_index("grp")
    rows_local = row_states.shape[0]
    full_rows = lax.all_gather(row_states, "mdl", axis=1, tiled=True)
    normed = rms_normalize(full_rows, ffn_gain)
    pre_active = jnp.dot(
        normed,
        lax.all_gather(ffn_in, "grp", axis=0, tiled=True),
        preferred_element_type=jnp.float32,
    )
    hidden = jnp.maximum(pre_active, 0.0).astype(jnp.bfloat16)
    ffn_terms = jnp.dot(
        hidden,
        lax.all_gather(ffn_out, "grp", axis=1, tiled=True),
        preferred_element_type=jnp.float32,
    )
    ffn_sum = lax.psum_scatter(ffn_terms, "mdl", scatter_dimension=1, tiled=True)
    enc_state = (row_states.astype(jnp.float32) + ffn_sum).astype(jnp.bfloat16)
    capacity, send_rows, send_valid, got_valid = bucket_plan(
        row_question, rows_local, groups, my_group
    )
    head_cols = kv_weight.shape[2]
    outgoing = pack_slots(enc_state, send_rows, send_valid)
    arrived = lax.all_to_all(outgoing, "grp", split_axis=0, concat_axis=0, tiled=True)
    slot_rows = lax.all_gather(arrived.reshape(groups * capacity, -1), "mdl", axis=1, tiled=True)
    encoded = rms_normalize(slot_rows, final_gain)
    projected = jnp.einsum(
        "rd,kdc->krc", encoded, kv_weight, preferred_element_type=jnp.float32
    ).astype(jnp.bfloat16)
    key_rows = projected[0]
    value_rows = projected[1]
    targets = queries.shape[0]
    heads_local = head_cols // HEAD_DIM
    query_heads = queries.reshape(targets, heads_local, HEAD_DIM)
    key_heads = key_rows.reshape(-1, heads_local, HEAD_DIM)
    value_heads = value_rows.reshape(-1, heads_local, HEAD_DIM)
    scores = jnp.einsum("thd,rhd->htr", query_heads, key_heads, preferred_element_type=jnp.float32)
    slot_mask = got_valid[None, None, :]
    scores = jnp.where(slot_mask, scores, -1e30)
    top_score = jnp.max(scores, axis=-1, keepdims=True)
    raised = jnp.where(slot_mask, jnp.exp(scores - top_score), 0.0)
    probabilities = (raised / jnp.sum(raised, axis=-1, keepdims=True)).astype(jnp.bfloat16)
    attended = jnp.einsum(
        "htr,rhd->thd", probabilities, value_heads, preferred_element_type=jnp.float32
    )
    attended = attended.astype(jnp.bfloat16).reshape(targets, head_cols)
    return lax.psum_scatter(
        jnp.dot(attended, attn_out, preferred_element_type=jnp.float32).astype(jnp.bfloat16),
        "mdl",
        scatter_dimension=0,
        tiled=True,
    )


def solution(mesh):
    in_specs = (
        P("grp", "mdl"),
        P(),
        P("grp", "mdl"),
        P("mdl", "grp"),
        P(),
        P(None, None, "mdl"),
        P("grp", "mdl"),
        P("mdl", None),
        P(),
    )
    out_specs = P(("grp", "mdl"), None)
    return jax.shard_map(local, mesh=mesh, in_specs=in_specs, out_specs=out_specs, check_vma=False)
```

profile of v0, /device:TPU:8, one launch (start us, length us, event | category | flops | bytes accessed | tf_op | source)
XLA Modules:
  0.0 669.9 jit_solution(2616351746955564816)
XLA Ops:
  6.5 0.0 copy-start
  6.5 0.0 all-gather.4.cloned.1.call-start
  6.5 0.7 all-gather.4.cloned.1.call-update
  7.3 0.0 all-gather.6.cloned.1.call-start
  7.3 0.7 all-gather.6.cloned.1.call-update
  8.0 0.0 reduce-scatter.3.cloned.1.call-start
  8.1 0.7 convert_element_type.51
  8.7 56.0 %all_gather.12 = bf16[384,1024]{0,1:T(8,128)(2,1)S(1)} all-gather(bf16[384,32]{0,1:T(8,128)(2,1)} %param.9), channel_id=1, replica_groups=mesh['grp'=16,'mdl'=32] {'mdl'}, dimensions={1}, use_global_device_ids=true | all-gather | bytes 811008 | tf_op jit(solution)/shard_map/all_gather | solution.py:46
  64.7 0.2 fusion.14
  64.9 0.0 copy-start.4
  64.9 0.0 all-gather.4.cloned.1.call-done
  65.0 33.6 %all-gather.6.cloned.1.call-done = bf16[1024,1024]{0,1:T(8,128)(2,1)} async-done(((bf16[1024,64]{0,1:T(8,128)(2,1)}), bf16[1024,1024]{0,1:T(8,128)(2,1)}) %all-gather.6.cloned.1.call-update) | async-done | bytes 2097168 | tf_op jit(solution)/shard_map/all_gather | solution.py:56
  98.5 5.6 fusion.22
  104.1 0.0 copy-start.3
  104.1 0.0 reduce-scatter.3.cloned.1.call-update
  104.1 0.0 all-gather.8.cloned.1.call-start
  104.2 0.0 copy-done.4
  104.2 0.4 convert_reduce_fusion
  104.6 0.2 reduce_window_sum.11
  104.8 0.1 add_minimum_fusion
  104.8 0.1 min.22
  104.9 0.1 iota_compare_fusion.2
  105.0 0.2 broadcast_in_dim.60
  105.2 0.2 broadcast_in_dim.61
  105.5 0.2 broadcast_in_dim.62
  105.7 0.2 broadcast_in_dim.63
  106.0 222.1 %reduce-scatter.3.cloned.1.call-done = f32[384,32]{0,1:T(8,128)} async-done(((f32[384,1024]{0,1:T(8,128)}), f32[384,32]{0,1:T(8,128)}) %reduce-scatter.3.cloned.1.call-update) | async-done | bytes 49168 | tf_op jit(solution)/shard_map/reduce_scatter | solution.py:59
  328.1 0.0 copy-done.3
  328.1 0.8 add_convert_fusion
  328.9 0.1 copy.28
  329.0 0.0 copy-start.5
  329.0 2.9 gather_fusion
  332.0 0.2 gather.7
  332.2 0.5 broadcast.116
  332.7 0.7 reduce.5
  333.4 13.6 %all_to_all.6 = bf16[16,2,1152]{2,1,0:T(2,128)(2,1)S(1)} all-to-all(bf16[16,2,1152]{2,1,0:T(2,128)(2,1)S(1)} %reshape.169), channel_id=1, replica_groups=mesh['grp'=16,'mdl'=32] {'grp'}, dimensions={0} | all-to-all | bytes 147456 | tf_op jit(solution)/shard_map/all_to_all | solution.py:66
  347.0 0.1 reshape.170
  347.0 0.4 reduce.1
  347.5 0.2 reshape.154
  347.7 0.8 copy.30
  348.5 0.0 all-gather.8.cloned.1.call-update
  348.5 0.0 reduce-scatter.5.cloned.1.call-start
  348.5 0.0 copy-done.5
  348.6 0.2 dynamic-slice_reduce_fusion
  348.7 0.1 iota_compare_fusion.1
  348.8 0.1 lt.86
  348.9 78.2 %all-gather.8.cloned.1.call-done = bf16[1152,1024]{0,1:T(8,128)(2,1)} async-done(((bf16[1152,32]{0,1:T(8,128)(2,1)}), bf16[1152,1024]{0,1:T(8,128)(2,1)}) %all-gather.8.cloned.1.call-update) | async-done | bytes 2359312 | tf_op jit(solution)/shard_map/all_gather | solution.py:67
  427.1 0.0 copy-start.1
  427.1 2.3 fusion.2
  429.4 0.0 copy-done
  429.4 0.0 copy-done.1
  429.5 3.5 fusion.8
  432.9 0.0 copy-start.6
  432.9 1.2 fusion.40
  434.2 0.0 copy-done.6
  434.2 5.5 fusion.41
  439.7 0.0 copy-start.2
  439.7 2.9 fusion.17
  442.6 0.0 copy-done.2
  442.6 1.3 convolution_convert_fusion.1
  443.9 0.0 reduce-scatter.5.cloned.1.call-update
  443.9 219.4 %reduce-scatter.5.cloned.1.call-done = bf16[8,1024]{1,0:T(8,128)(2,1)} async-done(((bf16[256,1024]{1,0:T(8,128)(2,1)}), bf16[8,1024]{1,0:T(8,128)(2,1)}) %reduce-scatter.5.cloned.1.call-update) | async-done | bytes 16400 | tf_op jit(solution)/shard_map/reduce_scatter | solution.py:89
  (9 shorter events, 0.1 us)
Async XLA Ops:
  6.5 422.9 %copy-start = (bf16[2,1024,512]{2,1,0:T(8,128)(2,1)S(1)}, bf16[2,1024,512]{2,1,0:T(8,128)(2,1)}, u32[]{:S(2)}) copy-start(bf16[2,1024,512]{2,1,0:T(8,128)(2,1)} %param.14) | copy-start | bytes 6291460
  6.5 58.4 %all-gather.4.cloned.1.call-start = ((), (), s32[]{:S(2)}) async-start(), calls=%async_computation.3 | async-start | bytes 2228224 | tf_op jit(solution)/shard_map/all_gather | solution.py:50
  7.3 91.3 %all-gather.6.cloned.1.call-start = ((), (), s32[]{:S(2)}) async-start(), calls=%async_computation.4 | async-start | bytes 2228224 | tf_op jit(solution)/shard_map/all_gather | solution.py:56
  8.0 320.1 %reduce-scatter.3.cloned.1.call-start = ((), (), s32[]{:S(2)}) async-start(), calls=%async_computation.5 | async-start | bytes 1622016 | tf_op jit(solution)/shard_map/reduce_scatter | solution.py:59
  64.9 39.3 %copy-start.4 = (s32[6144]{0:T(1024)S(1)}, s32[6144]{0:T(1024)}, u32[]{:S(2)}) copy-start(s32[6144]{0:T(1024)} %param.17) | copy-start | bytes 73732
  104.1 224.0 %copy-start.3 = (bf16[384,32]{0,1:T(8,128)(2,1)S(1)}, bf16[384,32]{0,1:T(8,128)(2,1)}, u32[]{:S(2)}) copy-start(bf16[384,32]{0,1:T(8,128)(2,1)} %param.9) | copy-start | bytes 73732
  104.1 322.9 %all-gather.8.cloned.1.call-start = ((), (), s32[]{:S(2)}) async-start(), calls=%async_computation.6 | async-start | bytes 2433024 | tf_op jit(solution)/shard_map/all_gather | solution.py:67
  329.0 19.5 %copy-start.5 = (bf16[1024]{0:T(1024)(128)(2,1)S(1)}, bf16[1024]{0:T(1024)(128)(2,1)}, u32[]{:S(2)}) copy-start(bf16[1024]{0:T(1024)(128)(2,1)} %param.13) | copy-start | bytes 6148
  348.5 314.8 %reduce-scatter.5.cloned.1.call-start = ((), (), s32[]{:S(2)}) async-start(), calls=%async_computation.7 | async-start | bytes 540672 | tf_op jit(solution)/shard_map/reduce_scatter | solution.py:89
  427.1 2.4 copy-start.1
  432.9 1.2 copy-start.6
  439.7 3.0 copy-start.2
Sparse Core Ops, SparseCore 0:
  9.5 46.1 all-gather.3
  57.7 40.7 all-gather.5
  104.3 223.7 reduce-scatter.2
  348.6 78.4 all-gather.7
  444.0 219.2 reduce-scatter.4
where the time goes:
time: 670 us
  waiting for transfers between devices  555 us (83%)
  blocking collectives  69.5 us (10%)
  matrix products  18.7 us (3%)
  between operations  13.3 us (2%)
  local copies, waits for them, and re-layouts  7.41 us (1%)
    reduce_scatter x1, waiting for transfers between devices, local(): lax.psum_scatter(ffn_terms, 'mdl', scatter_dimension=1, tiled=True)  222 us
    reduce_scatter x1, waiting for transfers between devices, local(): lax.psum_scatter(jnp.dot(attended, attn_out, preferred_element_type=jnp.f...  219 us
    all_gather x1, waiting for transfers between devices, local(): lax.all_gather(arrived.reshape(groups * capacity, -1), 'mdl', axis=1, til...  78.2 us
    all_gather x1, blocking collectives, local(): full_rows = lax.all_gather(row_states, 'mdl', axis=1, tiled=True)  56 us
    all_gather x1, waiting for transfers between devices, local(): lax.all_gather(ffn_out, 'grp', axis=1, tiled=True)  33.6 us
    all_to_all x1, blocking collectives, local(): lax.all_to_all(outgoing, 'grp', split_axis=0, concat_axis=0, tiled=True)  13.6 us
  transfers between devices with their start and end apart: 5, of which 4 were waited for; matrix products, arithmetic and copies ran while one was open for 0% of the time, Pallas kernels for 0%

commit v1 on v0

--- a/solution.py
+++ b/solution.py
@@ -43,7 +43,10 @@
     groups = lax.axis_size("grp")
     my_group = lax.axis_index("grp")
     rows_local = row_states.shape[0]
-    full_rows = lax.all_gather(row_states, "mdl", axis=1, tiled=True)
+    count = lax.axis_size("mdl")
+    shards = jnp.stack([row_states for _ in range(count)])
+    shards = lax.all_to_all(shards, "mdl", split_axis=0, concat_axis=0)
+    full_rows = jnp.concatenate(shards, axis=1)
     normed = rms_normalize(full_rows, ffn_gain)
     pre_active = jnp.dot(
         normed,

time: 670 us -> 670 us (level)
  blocking collectives: 69.5 us -> 13.6 us
  waiting for transfers between devices: 555 us -> 595 us
  starting transfers between devices: 0.16 us -> 13.3 us
    all_gather x1 -> x0, blocking collectives: 56 us -> none  [local(): full_rows = lax.all_gather(row_states, 'mdl', axis=1, tiled=True)]
    all_to_all x0 -> x1, waiting for transfers between devices: none -> 23.3 us  [local(): shards = lax.all_to_all(shards, 'mdl', split_axis=0, concat_axis=0)]
    all_to_all x0 -> x1, starting transfers between devices: none -> 13.2 us  [local(): shards = lax.all_to_all(shards, 'mdl', split_axis=0, concat_axis=0)]
    all_gather x1, waiting for transfers between devices: 33.6 us -> 43 us  [local(): lax.all_gather(ffn_out, 'grp', axis=1, tiled=True)]
    all_gather x1, waiting for transfers between devices: 0.02 us -> 7.94 us  [local(): lax.all_gather(ffn_in, 'grp', axis=0, tiled=True)]
  transfers between devices with their start and end apart: 5 -> 6, of which waited for: 4 -> 6; matrix products, arithmetic and copies ran while one was open for 0% -> 1% of each run, Pallas kernels for 0% -> 0%
where the time goes in v1:
time: 670 us
  waiting for transfers between devices  595 us (89%)
  matrix products  18.9 us (3%)
  blocking collectives  13.6 us (2%)
  starting transfers between devices  13.3 us (2%)
  between operations  13.3 us (2%)
  local copies, waits for them, and re-layouts  9.1 us (1%)
    reduce_scatter x1, waiting for transfers between devices, local(): lax.psum_scatter(ffn_terms, 'mdl', scatter_dimension=1, tiled=True)  222 us
    reduce_scatter x1, waiting for transfers between devices, local(): lax.psum_scatter(jnp.dot(attended, attn_out, preferred_element_type=jnp.f...  219 us
    all_gather x1, waiting for transfers between devices, local(): lax.all_gather(arrived.reshape(groups * capacity, -1), 'mdl', axis=1, til...  78.1 us
    all_gather x1, waiting for transfers between devices, local(): lax.all_gather(ffn_out, 'grp', axis=1, tiled=True)  43 us
    all_to_all x1, waiting for transfers between devices, local(): shards = lax.all_to_all(shards, 'mdl', split_axis=0, concat_axis=0)  23.3 us
    all_to_all x1, blocking collectives, local(): lax.all_to_all(outgoing, 'grp', split_axis=0, concat_axis=0, tiled=True)  13.6 us
  transfers between devices with their start and end apart: 6, of which 6 were waited for; matrix products, arithmetic and copies ran while one was open for 1% of the time, Pallas kernels for 0%

profile of v1, /device:TPU:8, one launch (start us, length us, event | category | flops | bytes accessed | tf_op | source)
XLA Modules:
  0.0 669.8 jit_solution(13014033615071384939)
XLA Ops:
  6.5 0.0 copy-start
  6.5 0.0 copy-start.5
  6.5 0.0 all-gather.4.cloned.1.call-start
  6.5 0.7 all-gather.4.cloned.1.call-update
  7.3 0.0 all-gather.6.cloned.1.call-start
  7.3 0.7 all-gather.6.cloned.1.call-update
  8.0 1.7 stack.2
  9.7 13.2 %all-to-all-start = ((bf16[32,384,32]{1,2,0:T(8,128)(2,1)}), bf16[32,384,32]{1,2,0:T(8,128)(2,1)S(1)}, u32[]{:S(2)}, u32[]{:S(2)}) async-start(bf16[32,384,32]{1,2,0:T(8,128)(2,1)} %stack.2), calls=%async_computation | async-start | bytes 1572864 | tf_op jit(solution)/shard_map/all_to_all | solution.py:48
  22.9 0.0 reduce-scatter.3.cloned.1.call-start
  22.9 0.0 copy-done.5
  22.9 23.3 %all-to-all-done = bf16[32,384,32]{1,2,0:T(8,128)(2,1)S(1)} async-done(((bf16[32,384,32]{1,2,0:T(8,128)(2,1)}), bf16[32,384,32]{1,2,0:T(8,128)(2,1)S(1)}, u32[]{:S(2)}, u32[]{:S(2)}) %all-to-all-start) | async-done | bytes 786464 | tf_op jit(solution)/shard_map/all_to_all | solution.py:48
  46.2 0.2 multiply_reduce_fusion
  46.5 1.1 fusion.15
  47.6 0.0 copy-start.4
  47.6 7.9 %all-gather.4.cloned.1.call-done = bf16[1024,1024]{1,0:T(8,128)(2,1)} async-done(((bf16[64,1024]{1,0:T(8,128)(2,1)}), bf16[1024,1024]{1,0:T(8,128)(2,1)}) %all-gather.4.cloned.1.call-update) | async-done | bytes 2097168 | tf_op jit(solution)/shard_map/all_gather | solution.py:53
  55.5 43.0 %all-gather.6.cloned.1.call-done = bf16[1024,1024]{0,1:T(8,128)(2,1)} async-done(((bf16[1024,64]{0,1:T(8,128)(2,1)}), bf16[1024,1024]{0,1:T(8,128)(2,1)}) %all-gather.6.cloned.1.call-update) | async-done | bytes 2097168 | tf_op jit(solution)/shard_map/all_gather | solution.py:59
  98.5 5.7 fusion.17
  104.3 0.0 copy-start.3
  104.3 0.0 reduce-scatter.3.cloned.1.call-update
  104.3 0.0 all-gather.8.cloned.1.call-start
  104.4 0.0 copy-done.4
  104.4 0.4 convert_reduce_fusion
  104.7 0.2 reduce_window_sum.11
  104.9 0.1 add_minimum_fusion
  105.0 0.1 min.22
  105.1 0.1 iota_compare_fusion.2
  105.2 0.2 broadcast_in_dim.60
  105.4 0.2 broadcast_in_dim.61
  105.6 0.2 broadcast_in_dim.62
  105.9 0.2 broadcast_in_dim.63
  106.1 222.2 %reduce-scatter.3.cloned.1.call-done = f32[384,32]{0,1:T(8,128)} async-done(((f32[384,1024]{0,1:T(8,128)}), f32[384,32]{0,1:T(8,128)}) %reduce-scatter.3.cloned.1.call-update) | async-done | bytes 49168 | tf_op jit(solution)/shard_map/reduce_scatter | solution.py:62
  328.3 0.0 copy-done.3
  328.3 0.8 add_convert_fusion
  329.1 0.1 copy.29
  329.2 0.0 copy-start.6
  329.2 2.9 gather_fusion
  332.2 0.2 gather.7
  332.4 0.5 broadcast.118
  332.9 0.7 reduce.7
  333.6 13.6 %all_to_all.11 = bf16[16,2,1152]{2,1,0:T(2,128)(2,1)S(1)} all-to-all(bf16[16,2,1152]{2,1,0:T(2,128)(2,1)S(1)} %reshape.176), channel_id=1, replica_groups=mesh['grp'=16,'mdl'=32] {'grp'}, dimensions={0} | all-to-all | bytes 147456 | tf_op jit(solution)/shard_map/all_to_all | solution.py:69
  347.2 0.1 reshape.177
  347.2 0.4 reduce.3
  347.7 0.2 reshape.160
  347.9 0.8 copy.31
  348.7 0.0 all-gather.8.cloned.1.call-update
  348.7 0.0 reduce-scatter.5.cloned.1.call-start
  348.7 0.0 copy-done.6
  348.8 0.2 dynamic-slice_reduce_fusion
  348.9 0.1 iota_compare_fusion.1
  349.0 0.1 lt.86
  349.1 78.1 %all-gather.8.cloned.1.call-done = bf16[1152,1024]{0,1:T(8,128)(2,1)} async-done(((bf16[1152,32]{0,1:T(8,128)(2,1)}), bf16[1152,1024]{0,1:T(8,128)(2,1)}) %all-gather.8.cloned.1.call-update) | async-done | bytes 2359312 | tf_op jit(solution)/shard_map/all_gather | solution.py:70
  427.3 2.3 fusion.2
  429.6 0.0 copy-done
  429.6 0.0 copy-done.1
  429.7 3.5 fusion.8
  433.1 0.0 copy-start.7
  433.1 1.2 fusion.34
  434.4 0.0 copy-done.7
  434.4 5.5 fusion.35
  439.8 3.0 fusion.16
  442.8 0.0 copy-done.2
  442.8 1.3 convolution_convert_fusion.1
  444.1 0.0 reduce-scatter.5.cloned.1.call-update
  444.1 219.2 %reduce-scatter.5.cloned.1.call-done = bf16[8,1024]{1,0:T(8,128)(2,1)} async-done(((bf16[256,1024]{1,0:T(8,128)(2,1)}), bf16[8,1024]{1,0:T(8,128)(2,1)}) %reduce-scatter.5.cloned.1.call-update) | async-done | bytes 16400 | tf_op jit(solution)/shard_map/reduce_scatter | solution.py:92
  (12 shorter events, 0.1 us)
Async XLA Ops:
  6.5 423.1 %copy-start = (bf16[2,1024,512]{2,1,0:T(8,128)(2,1)S(1)}, bf16[2,1024,512]{2,1,0:T(8,128)(2,1)}, u32[]{:S(2)}) copy-start(bf16[2,1024,512]{2,1,0:T(8,128)(2,1)} %param.14) | copy-start | bytes 6291460
  6.5 16.4 %copy-start.5 = (bf16[1024]{0:T(1024)(128)(2,1)S(1)}, bf16[1024]{0:T(1024)(128)(2,1)}, u32[]{:S(2)}) copy-start(bf16[1024]{0:T(1024)(128)(2,1)} %param.10) | copy-start | bytes 6148
  6.5 49.0 %all-gather.4.cloned.1.call-start = ((), (), s32[]{:S(2)}) async-start(), calls=%async_computation.4 | async-start | bytes 2228224 | tf_op jit(solution)/shard_map/all_gather | solution.py:53
  7.3 91.3 %all-gather.6.cloned.1.call-start = ((), (), s32[]{:S(2)}) async-start(), calls=%async_computation.5 | async-start | bytes 2228224 | tf_op jit(solution)/shard_map/all_gather | solution.py:59
  9.7 36.5 %all-to-all-start = ((bf16[32,384,32]{1,2,0:T(8,128)(2,1)}), bf16[32,384,32]{1,2,0:T(8,128)(2,1)S(1)}, u32[]{:S(2)}, u32[]{:S(2)}) async-start(bf16[32,384,32]{1,2,0:T(8,128)(2,1)} %stack.2), calls=%async_computation | async-start | bytes 1572864 | tf_op jit(solution)/shard_map/all_to_all | solution.py:48
  22.9 305.4 %reduce-scatter.3.cloned.1.call-start = ((), (), s32[]{:S(2)}) async-start(), calls=%async_computation.6 | async-start | bytes 1622016 | tf_op jit(solution)/shard_map/reduce_scatter | solution.py:62
  47.6 56.8 %copy-start.4 = (s32[6144]{0:T(1024)S(1)}, s32[6144]{0:T(1024)}, u32[]{:S(2)}) copy-start(s32[6144]{0:T(1024)} %param.17) | copy-start | bytes 73732
  104.3 224.0 %copy-start.3 = (bf16[384,32]{0,1:T(8,128)(2,1)S(1)}, bf16[384,32]{0,1:T(8,128)(2,1)}, u32[]{:S(2)}) copy-start(bf16[384,32]{0,1:T(8,128)(2,1)} %param.9) | copy-start | bytes 73732
  104.3 323.0 %all-gather.8.cloned.1.call-start = ((), (), s32[]{:S(2)}) async-start(), calls=%async_computation.7 | async-start | bytes 2433024 | tf_op jit(solution)/shard_map/all_gather | solution.py:70
  329.2 19.5 %copy-start.6 = (bf16[1024]{0:T(1024)(128)(2,1)S(1)}, bf16[1024]{0:T(1024)(128)(2,1)}, u32[]{:S(2)}) copy-start(bf16[1024]{0:T(1024)(128)(2,1)} %param.13) | copy-start | bytes 6148
  348.7 314.6 %reduce-scatter.5.cloned.1.call-start = ((), (), s32[]{:S(2)}) async-start(), calls=%async_computation.8 | async-start | bytes 540672 | tf_op jit(solution)/shard_map/reduce_scatter | solution.py:92
  427.3 2.4 copy-start.1
  433.1 1.2 copy-start.7
  439.8 3.0 copy-start.2
Sparse Core Ops, SparseCore 0:
  9.5 46.0 all-gather.3
  57.6 40.8 all-gather.5
  104.4 223.8 reduce-scatter.2
  348.8 78.4 all-gather.7
  444.2 218.9 reduce-scatter.4
